TPU v7x, 512 devices: a whole 4x8x8 slice. The times are simulated.
512 devices in a mesh: freq: 8 (over x, core), space: 64 (over z, y).
Axes of the slice: x: 4, y: 8, z: 8, core: 2. Of those that a mesh axis runs over, the one named last changes fastest.
Arguments:
- rhs: float32 [2, 5, 4096, 1024], P(None, None, ('freq', 'space')), parts along dimension 2, may hold values from -12 to 12
- inv_diag: float32 [2, 5, 5, 4096, 1024], P(None, None, None, ('freq', 'space')), parts along dimension 3
- face_coef: float32 [4, 4096, 1024], P(None, ('freq', 'space')), parts along dimension 1, may hold values from 0.6 to 1.8
- flux_jac: float32 [2, 5, 5], replicated, may hold values from -1.8 to 1.8
- press_weights: float32 [5], replicated, may hold values from -4 to 4
- surface_cells: int32 [32768], P('space'), may hold values from 0 to 8191, as said below
- interface_slot: int32 [32768], P('space'), may hold values from 0 to 32767, as said below
- mode_shapes: float32 [32768, 192], P('space'), may hold values from -0.09375 to 0.09375
Outputs:
- state: float32 [2, 5, 4096, 1024], P(None, None, ('freq', 'space')), parts along dimension 2
- forces: float32 [2, 1536], P(None, ('freq', 'space')), parts along dimension 1
There are 8 independent parts, one for each index of `freq`. A program takes and returns all parts, laid end to end along the dimension named above; an argument that names none is the same for every part. Nothing has to cross between parts.
Inputs may be any that keep to these rules, and one draw needn't show every extreme that they name: `surface_cells`: the 512 entries held by one device are distinct cell indices of that device; on some device they include both its first and its last cell. `interface_slot`: A permutation of all 32768 interface indices; the owner of index i is device i // 512 of space, and each device holds exactly the same number of rows of every owner.
All inputs are finite; a program needn't handle non-finite values.
Results may differ from a plain program's by a relative error of at most 0.0003.
Values sent between devices are 32-bit elements; how exact they have to be, the bound alone decides.
No kernel may reach another device: no remote copies, remote signals or barrier semaphores. Data moves between devices by JAX's collectives and lax.ppermute only.
A program may use at most 64 MiB of HBM per device.

v0:
```python
import jax
import jax.numpy as jnp
from jax import lax
from jax.sharding import PartitionSpec as P

ITERS = 8


def with_halo(block, sides, width):
    for axis, dim in sides:
        count = lax.axis_size(axis)
        forward = [(i, i + 1) for i in range(count - 1)]
        backward = [(target, source) for source, target in forward]
        low = lax.ppermute(
            lax.slice_in_dim(block, block.shape[dim] - width, None, axis=dim), axis, forward
        )
        high = lax.ppermute(lax.slice_in_dim(block, 0, width, axis=dim), axis, backward)
        block = jnp.concatenate([low, block, high], axis=dim)
    return block


def cut_along(value, dim, devices):
    before, after = (value.shape[:dim], value.shape[dim + 1 :])
    return jnp.moveaxis(value.reshape(*before, devices, -1, *after), dim, 0)


def summed_on_arrival(value, axis, dim):
    parts = cut_along(value, dim, lax.axis_size(axis))
    arrived = lax.all_to_all(parts, axis, split_axis=0, concat_axis=0, tiled=True)
    return arrived.sum(axis=0)


def block_apply(inv_diag, vector):
    real_part = jnp.sum(inv_diag[0] * vector[0][None], axis=1) - jnp.sum(
        inv_diag[1] * vector[1][None], axis=1
    )
    imag_part = jnp.sum(inv_diag[0] * vector[1][None], axis=1) + jnp.sum(
        inv_diag[1] * vector[0][None], axis=1
    )
    return jnp.stack([real_part, imag_part])


def couple(extended, face_coef, flux_jac):
    middle = extended[:, :, 1:-1, :]
    along_planes = face_coef[0] * extended[:, :, 2:, :] + face_coef[1] * extended[:, :, :-2, :]
    padded = jnp.pad(middle, ((0, 0), (0, 0), (0, 0), (1, 1)))
    along_cells = face_coef[2] * padded[..., 2:] + face_coef[3] * padded[..., :-2]
    mixed = jnp.einsum("kj,rjpq->rkpq", flux_jac[0], along_planes, precision=lax.Precision.HIGHEST)
    return mixed + jnp.einsum(
        "kj,rjpq->rkpq", flux_jac[1], along_cells, precision=lax.Precision.HIGHEST
    )


def sweep(extended, inv_diag, rhs, face_coef, flux_jac):
    return block_apply(inv_diag, rhs + couple(extended, face_coef, flux_jac))


def local(
    rhs, inv_diag, face_coef, flux_jac, press_weights, surface_cells, interface_slot, mode_shapes
):
    planes = rhs.shape[2]
    width_cells = rhs.shape[3]
    state = block_apply(inv_diag, rhs)
    for sweep_index in range(ITERS):
        extended = with_halo(state, (("space", 2),), 1)
        state = sweep(extended, inv_diag, rhs, face_coef, flux_jac)
    cells = state.reshape(2, 5, planes * width_cells)
    pressure = jnp.sum(press_weights[None, :, None] * cells, axis=1)
    surface = jnp.take(pressure, surface_cells, axis=1)
    row_count = interface_slot.shape[0]
    ranking = jnp.argsort(interface_slot)
    outgoing = jnp.take(surface, ranking, axis=1)
    local_index = (jnp.take(interface_slot, ranking) % row_count)[None]
    arrived, arrived_index = (
        lax.all_to_all(outgoing, "space", split_axis=1, concat_axis=1, tiled=True),
        lax.all_to_all(local_index, "space", split_axis=1, concat_axis=1, tiled=True),
    )
    placed = jnp.zeros((2, row_count), jnp.float32).at[:, arrived_index[0]].set(arrived)
    partial_forces = jnp.dot(
        placed, mode_shapes, precision=lax.Precision.HIGHEST, preferred_element_type=jnp.float32
    )
    forces = summed_on_arrival(partial_forces, "space", 1)
    return (state, forces)


def solution(mesh):
    in_specs = (
        P(None, None, ("freq", "space"), None),
        P(None, None, None, ("freq", "space"), None),
        P(None, ("freq", "space"), None),
        P(),
        P(),
        P("space"),
        P("space"),
        P("space", None),
    )
    out_specs = (P(None, None, ("freq", "space"), None), P(None, ("freq", "space")))
    return jax.shard_map(local, mesh=mesh, in_specs=in_specs, out_specs=out_specs, check_vma=False)
```

profile of v0, /device:TPU:6, one launch (start us, length us, event | category | flops | bytes accessed | tf_op | source)
XLA Modules:
  0.0 180.7 jit_solution(3756530067833134576)
XLA Ops:
  0.6 1.1 slice_bitcast_fusion.16
  1.8 1.7 fusion.17
  3.6 1.4 collective-permute-start
  5.0 4.5 %collective-permute-start.1 = (f32[2,5,1,1024]{3,2,1,0:T(1,128)S(1)}, f32[2,5,1,1024]{3,2,1,0:T(1,128)S(1)}, u32[]{:S(2)}, u32[]{:S(2)}) collective-permute-start(f32[2,5,1,1024]{3,2,1,0:T(1,128)S(1)} %get-tuple-element.107), channel_id=1, source_target_pairs={{0,1},{1,2},{2,3},{3,4},{4,5},{5,6},{6,7},{7,8},{8,9},{9,10},{10,1... | collective-permute-start | bytes 122888 | tf_op jit(solution)/shard_map/ppermute | solution.py:14
  9.7 3.8 %sort.17 = (s32[512]{0:T(512)}, s32[512]{0:T(512)S(1)}) sort(s32[512]{0:T(512)S(1)} %copy-done.1, s32[512]{0:T(512)S(1)} %iota.4), dimensions={0}, to_apply=%region_36.37 | sort | flops 4608 | bytes 8192 | tf_op jit(solution)/shard_map/jit(argsort)/sort | solution.py:71
  13.6 0.7 fusion.75
  14.6 0.9 fusion.15
  16.4 1.3 collective-permute-start.2
  17.7 4.5 %collective-permute-start.3 = (f32[2,5,1,1024]{3,2,1,0:T(1,128)S(1)}, f32[2,5,1,1024]{3,2,1,0:T(1,128)S(1)}, u32[]{:S(2)}, u32[]{:S(2)}) collective-permute-start(f32[2,5,1,1024]{3,2,1,0:T(1,128)S(1)} %get-tuple-element.103), channel_id=1, source_target_pairs={{0,1},{1,2},{2,3},{3,4},{4,5},{5,6},{6,7},{7,8},{8,9},{9,10},{10,1... | collective-permute-start | bytes 122888 | tf_op jit(solution)/shard_map/ppermute | solution.py:14
  22.3 1.6 collective-permute-done.3
  24.3 0.7 fusion.72
  25.1 0.9 fusion.13
  26.3 0.3 fusion.21
  26.7 1.3 collective-permute-start.4
  28.0 4.9 %collective-permute-start.5 = (f32[2,5,1,1024]{3,2,1,0:T(1,128)S(1)}, f32[2,5,1,1024]{3,2,1,0:T(1,128)S(1)}, u32[]{:S(2)}, u32[]{:S(2)}) collective-permute-start(f32[2,5,1,1024]{3,2,1,0:T(1,128)S(1)} %get-tuple-element.99), channel_id=1, source_target_pairs={{0,1},{1,2},{2,3},{3,4},{4,5},{5,6},{6,7},{7,8},{8,9},{9,10},{10,1... | collective-permute-start | bytes 122888 | tf_op jit(solution)/shard_map/ppermute | solution.py:14
  32.9 3.5 %gather_fusion = s32[512]{0:T(512)S(1)} fusion(s32[512]{0:T(512)S(1)} %copy-done.1, s32[1024]{0:T(1024)S(1)} %pad_clamp_fusion.1), kind=kCustom, calls=%fused_computation | custom fusion | bytes 6144 | tf_op jit(solution)/shard_map/jit(_take)/gather | solution.py:73
  36.8 0.7 fusion.69
  37.5 0.9 fusion.11
  38.7 0.3 fusion.23
  39.1 1.3 collective-permute-start.6
  40.4 4.7 %collective-permute-start.7 = (f32[2,5,1,1024]{3,2,1,0:T(1,128)S(1)}, f32[2,5,1,1024]{3,2,1,0:T(1,128)S(1)}, u32[]{:S(2)}, u32[]{:S(2)}) collective-permute-start(f32[2,5,1,1024]{3,2,1,0:T(1,128)S(1)} %get-tuple-element.95), channel_id=1, source_target_pairs={{0,1},{1,2},{2,3},{3,4},{4,5},{5,6},{6,7},{7,8},{8,9},{9,10},{10,1... | collective-permute-start | bytes 122888 | tf_op jit(solution)/shard_map/ppermute | solution.py:14
  45.3 1.4 collective-permute-done.7
  47.0 0.7 fusion.66
  47.8 0.9 fusion.9
  49.0 0.3 fusion.25
  49.3 1.3 collective-permute-start.8
  50.6 5.3 %collective-permute-start.9 = (f32[2,5,1,1024]{3,2,1,0:T(1,128)S(1)}, f32[2,5,1,1024]{3,2,1,0:T(1,128)S(1)}, u32[]{:S(2)}, u32[]{:S(2)}) collective-permute-start(f32[2,5,1,1024]{3,2,1,0:T(1,128)S(1)} %get-tuple-element.91), channel_id=1, source_target_pairs={{0,1},{1,2},{2,3},{3,4},{4,5},{5,6},{6,7},{7,8},{8,9},{9,10},{10,1... | collective-permute-start | bytes 122888 | tf_op jit(solution)/shard_map/ppermute | solution.py:14
  56.0 0.6 add_select_fusion
  56.6 27.3 %all-to-all-start = ((s32[1,64,8]{2,0,1:T(1,128)}), s32[1,64,8]{2,0,1:T(1,128)S(1)}, u32[]{:S(2)}, u32[]{:S(2)}) async-start(s32[1,64,8]{2,0,1:T(1,128)} %bitcast.58), calls=%async_computation | async-start | bytes 65536 | tf_op jit(solution)/shard_map/all_to_all | solution.py:76
  84.4 0.7 fusion.63
  85.1 0.9 fusion.7
  86.3 0.3 fusion.27
  86.7 1.3 collective-permute-start.10
  88.0 4.5 %collective-permute-start.11 = (f32[2,5,1,1024]{3,2,1,0:T(1,128)S(1)}, f32[2,5,1,1024]{3,2,1,0:T(1,128)S(1)}, u32[]{:S(2)}, u32[]{:S(2)}) collective-permute-start(f32[2,5,1,1024]{3,2,1,0:T(1,128)S(1)} %get-tuple-element.87), channel_id=1, source_target_pairs={{0,1},{1,2},{2,3},{3,4},{4,5},{5,6},{6,7},{7,8},{8,9},{9,10},{10,1... | collective-permute-start | bytes 122888 | tf_op jit(solution)/shard_map/ppermute | solution.py:14
  92.6 1.6 collective-permute-done.11
  94.6 0.7 fusion.60
  95.4 0.9 fusion.5
  96.6 0.3 fusion.29
  96.9 1.3 collective-permute-start.12
  98.2 5.1 %collective-permute-start.13 = (f32[2,5,1,1024]{3,2,1,0:T(1,128)S(1)}, f32[2,5,1,1024]{3,2,1,0:T(1,128)S(1)}, u32[]{:S(2)}, u32[]{:S(2)}) collective-permute-start(f32[2,5,1,1024]{3,2,1,0:T(1,128)S(1)} %get-tuple-element.83), channel_id=1, source_target_pairs={{0,1},{1,2},{2,3},{3,4},{4,5},{5,6},{6,7},{7,8},{8,9},{9,10},{10,1... | collective-permute-start | bytes 122888 | tf_op jit(solution)/shard_map/ppermute | solution.py:14
  103.4 1.4 collective-permute-done.13
  105.2 0.7 fusion.57
  105.9 0.9 fusion.3
  107.1 0.3 fusion.31
  107.5 1.3 collective-permute-start.14
  108.8 4.9 %collective-permute-start.15 = (f32[2,5,1,1024]{3,2,1,0:T(1,128)S(1)}, f32[2,5,1,1024]{3,2,1,0:T(1,128)S(1)}, u32[]{:S(2)}, u32[]{:S(2)}) collective-permute-start(f32[2,5,1,1024]{3,2,1,0:T(1,128)S(1)} %get-tuple-element.79), channel_id=1, source_target_pairs={{0,1},{1,2},{2,3},{3,4},{4,5},{5,6},{6,7},{7,8},{8,9},{9,10},{10,1... | collective-permute-start | bytes 122888 | tf_op jit(solution)/shard_map/ppermute | solution.py:14
  113.8 0.5 broadcast.113
  114.3 0.7 reduce.3
  115.7 0.7 fusion.54
  116.5 0.9 fusion.1
  118.6 2.6 %copy.151 = f32[2,8192]{0,1:T(8,128)} copy(f32[2,8192]{1,0:T(2,128)S(1)} %fusion.52) | data formatting | bytes 131072 | tf_op jit(solution)/shard_map/reduce_sum | solution.py:68
  121.2 3.2 %gather_fusion.1 = f32[512,2]{1,0:T(8,128)S(1)} fusion(f32[2,8192]{0,1:T(8,128)} %copy.151, s32[1024]{0:T(1024)S(1)} %pad_clamp_fusion), kind=kCustom, calls=%fused_computation.1 | custom fusion | bytes 10240 | tf_op jit(solution)/shard_map/jit(_take)/gather | solution.py:69
  124.5 1.0 gather_fusion.2
  125.6 0.4 copy.152
  126.0 0.7 broadcast_select_fusion
  126.7 20.8 %all-to-all-start.1 = ((f32[2,64,8]{2,0,1:T(2,128)}), f32[2,64,8]{2,0,1:T(2,128)S(1)}, u32[]{:S(2)}, u32[]{:S(2)}) async-start(f32[2,64,8]{2,0,1:T(2,128)} %broadcast_select_fusion), calls=%async_computation.1 | async-start | bytes 131072 | tf_op jit(solution)/shard_map/all_to_all | solution.py:75
  147.5 12.2 %all-to-all-done.1 = f32[2,64,8]{2,0,1:T(2,128)S(1)} async-done(((f32[2,64,8]{2,0,1:T(2,128)}), f32[2,64,8]{2,0,1:T(2,128)S(1)}, u32[]{:S(2)}, u32[]{:S(2)}) %all-to-all-start.1) | async-done | bytes 4128 | tf_op jit(solution)/shard_map/all_to_all | solution.py:75
  160.0 1.8 scatter_custom_fusion
  161.8 0.5 fusion.145
  162.5 0.7 copy.155
  163.2 4.6 %all-to-all-start.2 = ((f32[64,2,3]{2,1,0:T(2,128)}), f32[64,2,3]{2,1,0:T(2,128)S(1)}, u32[]{:S(2)}, u32[]{:S(2)}) async-start(f32[64,2,3]{2,1,0:T(2,128)} %copy.155), calls=%async_computation.2 | async-start | bytes 131072 | tf_op jit(solution)/shard_map/all_to_all | solution.py:29
  167.8 0.7 pad_maximum_fusion.40
  168.6 11.5 %all-to-all-done.2 = f32[64,2,3]{2,1,0:T(2,128)S(1)} async-done(((f32[64,2,3]{2,1,0:T(2,128)}), f32[64,2,3]{2,1,0:T(2,128)S(1)}, u32[]{:S(2)}, u32[]{:S(2)}) %all-to-all-start.2) | async-done | bytes 1568 | tf_op jit(solution)/shard_map/all_to_all | solution.py:29
  180.0 0.6 reduce_sum.379
  (117 shorter events, 8.3 us)
Async XLA Ops:
  0.6 161.2 %copy-start = (f32[512,192]{0,1:T(8,128)S(1)}, f32[512,192]{0,1:T(8,128)}, u32[]{:S(2)}) copy-start(f32[512,192]{0,1:T(8,128)} %param.15) | copy-start | bytes 1179652
  1.7 7.9 %copy-start.4 = (f32[4,8,1024]{2,1,0:T(8,128)S(1)}, f32[4,8,1024]{2,1,0:T(8,128)}, u32[]{:S(2)}) copy-start(f32[4,8,1024]{2,1,0:T(8,128)} %param.10) | copy-start | bytes 393220
  1.7 7.9 %copy-start.6 = (f32[2,5,5]{2,0,1:T(2,128)S(1)}, f32[2,5,5]{2,0,1:T(2,128)}, u32[]{:S(2)}) copy-start(f32[2,5,5]{2,0,1:T(2,128)} %param.11) | copy-start | bytes 604
  1.7 7.9 %copy-start.1 = (s32[512]{0:T(512)S(1)}, s32[512]{0:T(512)}, u32[]{:S(2)}) copy-start(s32[512]{0:T(512)} %param.14) | copy-start | bytes 6148
  3.6 11.0 %copy-start.3 = (f32[2,5,8,1024]{3,2,1,0:T(8,128)S(1)}, f32[2,5,8,1024]{3,2,1,0:T(8,128)}, u32[]{:S(2)}) copy-start(f32[2,5,8,1024]{3,2,1,0:T(8,128)} %param.8) | copy-start | bytes 983044
  3.6 9.8 %collective-permute-start = (f32[2,5,1,1024]{3,2,1,0:T(1,128)S(1)}, f32[2,5,1,1024]{3,2,1,0:T(1,128)S(1)}, u32[]{:S(2)}, u32[]{:S(2)}) collective-permute-start(f32[2,5,1,1024]{3,2,1,0:T(1,128)S(1)} %get-tuple-element.106), channel_id=1, source_target_pairs={{1,0},{2,1},{3,2},{4,3},{5,4},{6,5},{7,6},{8,7},{9,8},{10,9},{11,1... | collective-permute-start | bytes 122888 | tf_op jit(solution)/shard_map/ppermute | solution.py:17
  5.0 8.4 %collective-permute-start.1 = (f32[2,5,1,1024]{3,2,1,0:T(1,128)S(1)}, f32[2,5,1,1024]{3,2,1,0:T(1,128)S(1)}, u32[]{:S(2)}, u32[]{:S(2)}) collective-permute-start(f32[2,5,1,1024]{3,2,1,0:T(1,128)S(1)} %get-tuple-element.107), channel_id=1, source_target_pairs={{0,1},{1,2},{2,3},{3,4},{4,5},{5,6},{6,7},{7,8},{8,9},{9,10},{10,1... | collective-permute-start | bytes 122888 | tf_op jit(solution)/shard_map/ppermute | solution.py:14
  14.6 1.4 copy-start.2
  16.4 5.9 %collective-permute-start.2 = (f32[2,5,1,1024]{3,2,1,0:T(1,128)S(1)}, f32[2,5,1,1024]{3,2,1,0:T(1,128)S(1)}, u32[]{:S(2)}, u32[]{:S(2)}) collective-permute-start(f32[2,5,1,1024]{3,2,1,0:T(1,128)S(1)} %get-tuple-element.102), channel_id=1, source_target_pairs={{1,0},{2,1},{3,2},{4,3},{5,4},{6,5},{7,6},{8,7},{9,8},{10,9},{11,1... | collective-permute-start | bytes 122888 | tf_op jit(solution)/shard_map/ppermute | solution.py:17
  17.7 6.2 %collective-permute-start.3 = (f32[2,5,1,1024]{3,2,1,0:T(1,128)S(1)}, f32[2,5,1,1024]{3,2,1,0:T(1,128)S(1)}, u32[]{:S(2)}, u32[]{:S(2)}) collective-permute-start(f32[2,5,1,1024]{3,2,1,0:T(1,128)S(1)} %get-tuple-element.103), channel_id=1, source_target_pairs={{0,1},{1,2},{2,3},{3,4},{4,5},{5,6},{6,7},{7,8},{8,9},{9,10},{10,1... | collective-permute-start | bytes 122888 | tf_op jit(solution)/shard_map/ppermute | solution.py:14
  26.7 9.7 %collective-permute-start.4 = (f32[2,5,1,1024]{3,2,1,0:T(1,128)S(1)}, f32[2,5,1,1024]{3,2,1,0:T(1,128)S(1)}, u32[]{:S(2)}, u32[]{:S(2)}) collective-permute-start(f32[2,5,1,1024]{3,2,1,0:T(1,128)S(1)} %get-tuple-element.98), channel_id=1, source_target_pairs={{1,0},{2,1},{3,2},{4,3},{5,4},{6,5},{7,6},{8,7},{9,8},{10,9},{11,1... | collective-permute-start | bytes 122888 | tf_op jit(solution)/shard_map/ppermute | solution.py:17
  28.0 8.4 %collective-permute-start.5 = (f32[2,5,1,1024]{3,2,1,0:T(1,128)S(1)}, f32[2,5,1,1024]{3,2,1,0:T(1,128)S(1)}, u32[]{:S(2)}, u32[]{:S(2)}) collective-permute-start(f32[2,5,1,1024]{3,2,1,0:T(1,128)S(1)} %get-tuple-element.99), channel_id=1, source_target_pairs={{0,1},{1,2},{2,3},{3,4},{4,5},{5,6},{6,7},{7,8},{8,9},{9,10},{10,1... | collective-permute-start | bytes 122888 | tf_op jit(solution)/shard_map/ppermute | solution.py:14
  39.1 6.1 %collective-permute-start.6 = (f32[2,5,1,1024]{3,2,1,0:T(1,128)S(1)}, f32[2,5,1,1024]{3,2,1,0:T(1,128)S(1)}, u32[]{:S(2)}, u32[]{:S(2)}) collective-permute-start(f32[2,5,1,1024]{3,2,1,0:T(1,128)S(1)} %get-tuple-element.94), channel_id=1, source_target_pairs={{1,0},{2,1},{3,2},{4,3},{5,4},{6,5},{7,6},{8,7},{9,8},{10,9},{11,1... | collective-permute-start | bytes 122888 | tf_op jit(solution)/shard_map/ppermute | solution.py:17
  40.4 6.2 %collective-permute-start.7 = (f32[2,5,1,1024]{3,2,1,0:T(1,128)S(1)}, f32[2,5,1,1024]{3,2,1,0:T(1,128)S(1)}, u32[]{:S(2)}, u32[]{:S(2)}) collective-permute-start(f32[2,5,1,1024]{3,2,1,0:T(1,128)S(1)} %get-tuple-element.95), channel_id=1, source_target_pairs={{0,1},{1,2},{2,3},{3,4},{4,5},{5,6},{6,7},{7,8},{8,9},{9,10},{10,1... | collective-permute-start | bytes 122888 | tf_op jit(solution)/shard_map/ppermute | solution.py:14
  49.3 34.6 %collective-permute-start.8 = (f32[2,5,1,1024]{3,2,1,0:T(1,128)S(1)}, f32[2,5,1,1024]{3,2,1,0:T(1,128)S(1)}, u32[]{:S(2)}, u32[]{:S(2)}) collective-permute-start(f32[2,5,1,1024]{3,2,1,0:T(1,128)S(1)} %get-tuple-element.90), channel_id=1, source_target_pairs={{1,0},{2,1},{3,2},{4,3},{5,4},{6,5},{7,6},{8,7},{9,8},{10,9},{11,1... | collective-permute-start | bytes 122888 | tf_op jit(solution)/shard_map/ppermute | solution.py:17
  50.6 33.3 %collective-permute-start.9 = (f32[2,5,1,1024]{3,2,1,0:T(1,128)S(1)}, f32[2,5,1,1024]{3,2,1,0:T(1,128)S(1)}, u32[]{:S(2)}, u32[]{:S(2)}) collective-permute-start(f32[2,5,1,1024]{3,2,1,0:T(1,128)S(1)} %get-tuple-element.91), channel_id=1, source_target_pairs={{0,1},{1,2},{2,3},{3,4},{4,5},{5,6},{6,7},{7,8},{8,9},{9,10},{10,1... | collective-permute-start | bytes 122888 | tf_op jit(solution)/shard_map/ppermute | solution.py:14
  56.6 57.2 %all-to-all-start = ((s32[1,64,8]{2,0,1:T(1,128)}), s32[1,64,8]{2,0,1:T(1,128)S(1)}, u32[]{:S(2)}, u32[]{:S(2)}) async-start(s32[1,64,8]{2,0,1:T(1,128)} %bitcast.58), calls=%async_computation | async-start | bytes 65536 | tf_op jit(solution)/shard_map/all_to_all | solution.py:76
  86.3 6.3 %copy-start.5 = (s32[512]{0:T(512)S(1)}, s32[512]{0:T(512)}, u32[]{:S(2)}) copy-start(s32[512]{0:T(512)} %param.13) | copy-start | bytes 6148
  86.7 5.9 %collective-permute-start.10 = (f32[2,5,1,1024]{3,2,1,0:T(1,128)S(1)}, f32[2,5,1,1024]{3,2,1,0:T(1,128)S(1)}, u32[]{:S(2)}, u32[]{:S(2)}) collective-permute-start(f32[2,5,1,1024]{3,2,1,0:T(1,128)S(1)} %get-tuple-element.86), channel_id=1, source_target_pairs={{1,0},{2,1},{3,2},{4,3},{5,4},{6,5},{7,6},{8,7},{9,8},{10,9},{11,1... | collective-permute-start | bytes 122888 | tf_op jit(solution)/shard_map/ppermute | solution.py:17
  88.0 6.2 %collective-permute-start.11 = (f32[2,5,1,1024]{3,2,1,0:T(1,128)S(1)}, f32[2,5,1,1024]{3,2,1,0:T(1,128)S(1)}, u32[]{:S(2)}, u32[]{:S(2)}) collective-permute-start(f32[2,5,1,1024]{3,2,1,0:T(1,128)S(1)} %get-tuple-element.87), channel_id=1, source_target_pairs={{0,1},{1,2},{2,3},{3,4},{4,5},{5,6},{6,7},{7,8},{8,9},{9,10},{10,1... | collective-permute-start | bytes 122888 | tf_op jit(solution)/shard_map/ppermute | solution.py:14
  96.9 6.4 %collective-permute-start.12 = (f32[2,5,1,1024]{3,2,1,0:T(1,128)S(1)}, f32[2,5,1,1024]{3,2,1,0:T(1,128)S(1)}, u32[]{:S(2)}, u32[]{:S(2)}) collective-permute-start(f32[2,5,1,1024]{3,2,1,0:T(1,128)S(1)} %get-tuple-element.82), channel_id=1, source_target_pairs={{1,0},{2,1},{3,2},{4,3},{5,4},{6,5},{7,6},{8,7},{9,8},{10,9},{11,1... | collective-permute-start | bytes 122888 | tf_op jit(solution)/shard_map/ppermute | solution.py:17
  98.2 6.5 %collective-permute-start.13 = (f32[2,5,1,1024]{3,2,1,0:T(1,128)S(1)}, f32[2,5,1,1024]{3,2,1,0:T(1,128)S(1)}, u32[]{:S(2)}, u32[]{:S(2)}) collective-permute-start(f32[2,5,1,1024]{3,2,1,0:T(1,128)S(1)} %get-tuple-element.83), channel_id=1, source_target_pairs={{0,1},{1,2},{2,3},{3,4},{4,5},{5,6},{6,7},{7,8},{8,9},{9,10},{10,1... | collective-permute-start | bytes 122888 | tf_op jit(solution)/shard_map/ppermute | solution.py:14
  107.5 7.6 %collective-permute-start.14 = (f32[2,5,1,1024]{3,2,1,0:T(1,128)S(1)}, f32[2,5,1,1024]{3,2,1,0:T(1,128)S(1)}, u32[]{:S(2)}, u32[]{:S(2)}) collective-permute-start(f32[2,5,1,1024]{3,2,1,0:T(1,128)S(1)} %get-tuple-element.78), channel_id=1, source_target_pairs={{1,0},{2,1},{3,2},{4,3},{5,4},{6,5},{7,6},{8,7},{9,8},{10,9},{11,1... | collective-permute-start | bytes 122888 | tf_op jit(solution)/shard_map/ppermute | solution.py:17
  108.8 6.5 %collective-permute-start.15 = (f32[2,5,1,1024]{3,2,1,0:T(1,128)S(1)}, f32[2,5,1,1024]{3,2,1,0:T(1,128)S(1)}, u32[]{:S(2)}, u32[]{:S(2)}) collective-permute-start(f32[2,5,1,1024]{3,2,1,0:T(1,128)S(1)} %get-tuple-element.79), channel_id=1, source_target_pairs={{0,1},{1,2},{2,3},{3,4},{4,5},{5,6},{6,7},{7,8},{8,9},{9,10},{10,1... | collective-permute-start | bytes 122888 | tf_op jit(solution)/shard_map/ppermute | solution.py:14
  117.7 0.7 copy-start.7
  126.7 33.0 %all-to-all-start.1 = ((f32[2,64,8]{2,0,1:T(2,128)}), f32[2,64,8]{2,0,1:T(2,128)S(1)}, u32[]{:S(2)}, u32[]{:S(2)}) async-start(f32[2,64,8]{2,0,1:T(2,128)} %broadcast_select_fusion), calls=%async_computation.1 | async-start | bytes 131072 | tf_op jit(solution)/shard_map/all_to_all | solution.py:75
  163.2 16.9 %all-to-all-start.2 = ((f32[64,2,3]{2,1,0:T(2,128)}), f32[64,2,3]{2,1,0:T(2,128)S(1)}, u32[]{:S(2)}, u32[]{:S(2)}) async-start(f32[64,2,3]{2,1,0:T(2,128)} %copy.155), calls=%async_computation.2 | async-start | bytes 131072 | tf_op jit(solution)/shard_map/all_to_all | solution.py:29
where the time goes:
time: 181 us
  starting transfers between devices  102 us (56%)
  waiting for transfers between devices  30 us (17%)
  local copies, waits for them, and re-layouts  18.1 us (10%)
  other arithmetic  15.4 us (9%)
  matrix products  13.9 us (8%)
    ppermute x8, starting transfers between devices, with_halo(): lax.ppermute(lax.slice_in_dim(block, block.shape[dim] - width, None, axis...  38.5 us
    all_to_all x1, starting transfers between devices, local(): lax.all_to_all(local_index, 'space', split_axis=1, concat_axis=1, tiled=T...  27.3 us
    all_to_all x1, starting transfers between devices, local(): lax.all_to_all(outgoing, 'space', split_axis=1, concat_axis=1, tiled=True)  20.8 us
    all_to_all x1, waiting for transfers between devices, local(): lax.all_to_all(outgoing, 'space', split_axis=1, concat_axis=1, tiled=True)  12.2 us
    all_to_all x1, waiting for transfers between devices, summed_on_arrival(): lax.all_to_all(parts, axis, split_axis=0, concat_axis=0, tiled=True)  11.5 us
    ppermute x8, starting transfers between devices, with_halo(): lax.ppermute(lax.slice_in_dim(block, 0, width, axis=dim), axis, backward)  10.5 us
    dot_general x8, matrix products, couple(): jnp.einsum('kj,rjpq->rkpq', flux_jac[1], along_cells, precision=lax.Preci...  7.37 us
    ppermute x8, waiting for transfers between devices, with_halo(): lax.ppermute(lax.slice_in_dim(block, block.shape[dim] - width, None, axis...  6.19 us
  transfers between devices with their start and end apart: 19, of which 7 were waited for; matrix products, arithmetic and copies ran while one was open for 10% of the time, Pallas kernels for 0%

commit v1 on v0

v1 whole, which is shorter than its diff:
```python
import jax
import jax.numpy as jnp
from jax import lax
from jax.experimental import pallas as pl
from jax.experimental.pallas import tpu as pltpu
from jax.sharding import PartitionSpec as P

INTERPRET = False
HI = lax.Precision.HIGHEST
F32 = jnp.float32
BLK = 50
RHS = 50
FAC = 60
NF = 64
LANES = 128
MIB = 1 << 20


def tile_iota(dim):
    return lax.broadcasted_iota(jnp.int32, (8, LANES), dim)


def matvec(blk, vec):
    out = []
    for r in range(2):
        for k in range(5):
            acc = None
            for j in range(5):
                br, bi = blk(k * 5 + j), blk(25 + k * 5 + j)
                if r == 0:
                    term = br * vec[j] - bi * vec[5 + j]
                else:
                    term = br * vec[5 + j] + bi * vec[j]
                acc = term if acc is None else acc + term
            out.append(acc)
    return out


def next_cell(x):
    rolled = pltpu.roll(x, LANES - 1, 1)
    return jnp.where(tile_iota(1) == LANES - 1, pltpu.roll(rolled, 7, 0), rolled)


def prev_cell(x):
    rolled = pltpu.roll(x, 1, 1)
    return jnp.where(tile_iota(1) == 0, pltpu.roll(rolled, 1, 0), rolled)


def start_state(cx, st, plane):
    c, e = plane + 2, plane + 3
    new = matvec(lambda f: cx[f, c], [cx[RHS + f, c] for f in range(10)])
    for f in range(10):
        st[f, e] = new[f]


def advance(cx, st, flux, level, plane, out=None):
    c, e = plane + 2, plane + 3
    base = (level - 1) * 10
    f0, f1, f2, f3 = [cx[FAC + n, c] for n in range(4)]
    last = (tile_iota(0) == 7) & (tile_iota(1) == LANES - 1)
    first = (tile_iota(0) == 0) & (tile_iota(1) == 0)
    f2 = jnp.where(last, 0.0, f2)
    f3 = jnp.where(first, 0.0, f3)
    vec = []
    for r in range(2):
        across, along = [], []
        for j in range(5):
            n = base + r * 5 + j
            here = st[n, e]
            across.append(f0 * st[n, e + 1] + f1 * st[n, e - 1])
            along.append(f2 * next_cell(here) + f3 * prev_cell(here))
        for k in range(5):
            acc = cx[RHS + r * 5 + k, c]
            for j in range(5):
                acc = acc + flux[0, k, j] * across[j]
            for j in range(5):
                acc = acc + flux[1, k, j] * along[j]
            vec.append(acc)
    new = matvec(lambda f: cx[f, c], vec)
    for f in range(10):
        if out is None:
            st[level * 10 + f, e] = new[f]
        else:
            out[f, plane] = new[f]


def run(planes, body):
    for low, high in planes:
        if low == high:
            body(low)
        else:

            @pl.loop(low, high + 1)
            def _(plane):
                body(plane)


def plane_copies(source, target, sems, first, count, offset, at):
    copies = []
    for j in range(8):
        copies.append(
            pltpu.make_async_copy(
                source.at[:, first : first + count, j * LANES : (j + 1) * LANES],
                target.at[offset : offset + source.shape[0], at : at + count, j, :],
                sems,
            )
        )
    return copies


def pack_kernel(rhs, inv, face, low, high, edge, sems):
    copies = []
    for side, (target, first, inner) in enumerate(((low, 0, 2), (high, 6, 5))):
        copies += plane_copies(inv, target, sems.at[side], first, 2, 0, 0)
        copies += plane_copies(rhs, target, sems.at[side], first, 2, RHS, 0)
        copies += plane_copies(face, target, sems.at[side], first, 2, FAC, 0)
        copies += plane_copies(inv, edge, sems.at[side], inner, 1, 0, side)
        copies += plane_copies(rhs, edge, sems.at[side], inner, 1, RHS, side)
    for copy in copies:
        copy.start()
    for copy in copies:
        copy.wait()
    for side, target in enumerate((low, high)):
        new = matvec(lambda f: edge[f, side], [edge[RHS + f, side] for f in range(10)])
        for f in range(10):
            target[NF + f // 2, f % 2] = new[f]


def inner_kernel(flux, rhs, inv, face, cx, st, sems):
    copies = (
        plane_copies(inv, cx, sems.at[0], 0, 8, 0, 2)
        + plane_copies(rhs, cx, sems.at[0], 0, 8, RHS, 2)
        + plane_copies(face, cx, sems.at[0], 0, 8, FAC, 2)
    )
    for copy in copies:
        copy.start()
    for copy in copies:
        copy.wait()
    run([(0, 7)], lambda p: start_state(cx, st, p))
    for level in (1, 2, 3):
        run([(level, 7 - level)], lambda p: advance(cx, st, flux, level, p))


def middle_kernel(flux, got_low, got_high, cx_in, st_in, cx, st, low, high):
    del cx_in, st_in
    @pl.loop(0, NF)
    def _(f):
        for p in range(2):
            cx[f, p] = got_low[f, p]
            cx[f, 10 + p] = got_high[f, p]

    for f in range(10):
        st[f, 0] = got_low[NF + f // 2, f % 2]
        st[f, 13] = got_high[NF + f // 2, f % 2]
    run([(-2, -1), (8, 9)], lambda p: start_state(cx, st, p))
    for level in (1, 2, 3):
        run([(level - 3, level - 1), (8 - level, 10 - level)], lambda p: advance(cx, st, flux, level, p))
    run([(1, 6)], lambda p: advance(cx, st, flux, 4, p))
    run([(2, 5)], lambda p: advance(cx, st, flux, 5, p))
    run([(3, 4)], lambda p: advance(cx, st, flux, 6, p))
    for n, (level, low_plane, high_plane) in enumerate(EDGES):
        for f in range(10):
            low[n * 10 + f] = st[level * 10 + f, low_plane + 3]
            high[n * 10 + f] = st[level * 10 + f, high_plane + 3]


EDGES = ((3, 0, 6), (3, 1, 7), (4, 1, 5), (4, 2, 6), (5, 2, 5))


def last_kernel(
    flux, weights, got_low, got_high, cx, st_in, hit_row, hit_lane, spot, extra, owner_hit, st, out, packet, final, sems
):
    del st_in
    for n, (level, low_plane, high_plane) in enumerate(EDGES):
        for f in range(10):
            st[level * 10 + f, low_plane + 8 + 3] = got_high[n * 10 + f]
            st[level * 10 + f, high_plane - 8 + 3] = got_low[n * 10 + f]
    run([(-1, 0), (7, 8)], lambda p: advance(cx, st, flux, 4, p))
    run([(-2, 1), (6, 9)], lambda p: advance(cx, st, flux, 5, p))
    run([(-2, 2), (5, 9)], lambda p: advance(cx, st, flux, 6, p))
    run([(-1, 8)], lambda p: advance(cx, st, flux, 7, p))
    run([(0, 7)], lambda p: advance(cx, st, flux, 8, p, out=final))
    copies = [
        pltpu.make_async_copy(final.at[:, :, j, :], out.at[:, :, j * LANES : (j + 1) * LANES], sems.at[0])
        for j in range(8)
    ]
    for copy in copies:
        copy.start()
    press = []
    for r in range(2):
        acc = None
        for j in range(5):
            term = weights[j] * final[r * 5 + j].reshape(64, LANES)
            acc = term if acc is None else acc + term
        press.append(acc)
    rows = hit_row[...]
    lanes = hit_lane[...]
    value = []
    for r in range(2):
        picked = jnp.dot(rows, press[r], precision=HI, preferred_element_type=F32)
        value.append(jnp.sum(picked * lanes, axis=1, keepdims=True))
    column = lax.broadcasted_iota(jnp.int32, spot.shape, 1)
    routed = jnp.where(column < 8, value[0], value[1]) * spot[...] + extra[...]
    packet[...] = jnp.dot(owner_hit[...], routed, precision=HI, preferred_element_type=F32)
    for copy in copies:
        copy.wait()


def as_column(row):
    return jnp.broadcast_to(row.astype(F32), (LANES, row.shape[1])).T.astype(jnp.int32)


def route_kernel(slot_row, cell_row, hit_row, hit_lane, spot, extra, owner_hit):
    rows = slot_row.shape[1]
    owners = owner_hit.shape[0]
    slots = as_column(slot_row[...])
    slot_owner = slots // rows
    owner_col = slot_owner[:, 0:1]
    owner_row = slot_row[...] // rows
    before = lax.broadcasted_iota(jnp.int32, (rows, rows), 1) < lax.broadcasted_iota(jnp.int32, (rows, rows), 0)
    earlier = jnp.where((owner_col == owner_row) & before, 1.0, 0.0)
    position = jnp.sum(earlier, axis=1, keepdims=True).astype(jnp.int32)
    lane = lax.broadcasted_iota(jnp.int32, (rows, LANES), 1)
    here = (lane % 8) == position
    spot[...] = jnp.where(here & (lane < 16), 1.0, 0.0)
    local = (slots - slot_owner * rows).astype(F32)
    extra[...] = jnp.where(here & (lane >= 16) & (lane < 24), local, 0.0)
    owner_hit[...] = jnp.where(lax.broadcasted_iota(jnp.int32, (owners, rows), 0) == owner_row, 1.0, 0.0)
    cells = as_column(cell_row[...])
    hit_row[...] = jnp.where(lane == cells // LANES, 1.0, 0.0)[:, 0:64]
    hit_lane[...] = jnp.where(lane == cells % LANES, 1.0, 0.0)


def force_kernel(arrived, modes_t, shares):
    count = modes_t.shape[1]
    places = lax.broadcasted_iota(jnp.int32, (64, count), 1)
    got = arrived[...]
    re = jnp.zeros((64, count), F32)
    im = jnp.zeros((64, count), F32)
    for i in range(8):
        hit = got[:, 16 + i : 17 + i].astype(jnp.int32) == places
        re = jnp.where(hit, got[:, i : i + 1], re)
        im = jnp.where(hit, got[:, 8 + i : 9 + i], im)
    re = jnp.sum(re, axis=0, keepdims=True)
    im = jnp.sum(im, axis=0, keepdims=True)
    both = jnp.where(lax.broadcasted_iota(jnp.int32, (8, count), 0) < 3, re, im)
    force = lax.dot_general(modes_t[...], both, (((1,), (1,)), ((), ())), precision=HI, preferred_element_type=F32)
    mode = lax.broadcasted_iota(jnp.int32, force.shape, 0)
    column = lax.broadcasted_iota(jnp.int32, force.shape, 1)
    kept = jnp.where((mode % 3 == column % 3) & (column < 6), force, 0.0)
    modes_n = force.shape[0]
    owner = lax.broadcasted_iota(jnp.int32, (64, modes_n), 0)
    mine = jnp.where(lax.broadcasted_iota(jnp.int32, (64, modes_n), 1) // 3 == owner, 1.0, 0.0)
    shares[...] = jnp.zeros(shares.shape, F32)
    shares[:, 0:8] = jnp.dot(mine, kept, precision=HI, preferred_element_type=F32)


def total_kernel(arrived, forces):
    total = jnp.sum(arrived[...], axis=0, keepdims=True)
    forces[0:1, :] = total[:, 0:3]
    forces[1:2, :] = total[:, 3:6]


def call(kernel, outs, ins, scratch=(), aliases=None, cost=None, vmem=24 * MIB):
    return pl.pallas_call(
        kernel,
        out_shape=[jax.ShapeDtypeStruct(shape, F32) for shape, _ in outs],
        in_specs=[pl.BlockSpec(memory_space=space) for _, space in ins],
        out_specs=[pl.BlockSpec(memory_space=space) for _, space in outs],
        scratch_shapes=list(scratch),
        input_output_aliases=aliases or {},
        compiler_params=pltpu.CompilerParams(vmem_limit_bytes=vmem),
        cost_estimate=pl.CostEstimate(flops=cost or 1000000, bytes_accessed=1000, transcendentals=0),
        interpret=INTERPRET,
    )(*[array for array, _ in ins])


V, S, A = pltpu.VMEM, pltpu.SMEM, pl.ANY


def exchange(low, high):
    count = lax.axis_size("space")
    up = [(i, i + 1) for i in range(count - 1)]
    down = [(target, source) for source, target in up]
    return lax.ppermute(high, "space", up), lax.ppermute(low, "space", down)


def local(rhs, inv_diag, face_coef, flux_jac, press_weights, surface_cells, interface_slot, mode_shapes):
    rhs_f = pltpu.with_memory_space_constraint(rhs.reshape(10, 8, 1024), pltpu.HBM)
    inv_f = pltpu.with_memory_space_constraint(inv_diag.reshape(50, 8, 1024), pltpu.HBM)
    face_coef = pltpu.with_memory_space_constraint(face_coef, pltpu.HBM)
    flux = flux_jac
    rows = interface_slot.shape[0]
    dma = pltpu.SemaphoreType.DMA

    low, high = call(
        pack_kernel,
        [((NF + 5, 2, 8, LANES), V)] * 2,
        [(rhs_f, A), (inv_f, A), (face_coef, A)],
        [pltpu.VMEM((60, 2, 8, LANES), F32), dma((2,))],
    )
    got_low, got_high = exchange(low, high)

    hit_row, hit_lane, spot, extra, owner_hit = call(
        route_kernel,
        [((rows, 64), V), ((rows, LANES), V), ((rows, LANES), V), ((rows, LANES), V), ((64, rows), V)],
        [(interface_slot.reshape(1, rows), V), (surface_cells.reshape(1, rows), V)],
    )
    cx, st = call(
        inner_kernel,
        [((NF, 12, 8, LANES), V), ((80, 14, 8, LANES), V)],
        [(flux, S), (rhs_f, A), (inv_f, A), (face_coef, A)],
        [dma((1,))],
    )
    cx, st, low, high = call(
        middle_kernel,
        [((NF, 12, 8, LANES), V), ((80, 14, 8, LANES), V), ((50, 8, LANES), V), ((50, 8, LANES), V)],
        [(flux, S), (got_low, V), (got_high, V), (cx, V), (st, V)],
        aliases={3: 0, 4: 1},
    )
    got_low, got_high = exchange(low, high)
    _, state, packet = call(
        last_kernel,
        [((80, 14, 8, LANES), V), ((10, 8, 1024), A), ((64, LANES), V)],
        [(flux, S), (press_weights, S), (got_low, V), (got_high, V), (cx, V), (st, V), (hit_row, V), (hit_lane, V), (spot, V), (extra, V), (owner_hit, V)],
        [pltpu.VMEM((10, 8, 8, LANES), F32), dma((1,))],
        aliases={5: 0},
    )
    arrived = lax.all_to_all(packet.reshape(64, 1, LANES), "space", 0, 0, tiled=True)
    (shares,) = call(force_kernel, [((64, LANES), V)], [(arrived.reshape(64, LANES), V), (mode_shapes.T, V)])
    arrived = lax.all_to_all(shares.reshape(64, 1, LANES), "space", 0, 0, tiled=True)
    (forces,) = call(total_kernel, [((2, 3), V)], [(arrived.reshape(64, LANES), V)])
    return state.reshape(2, 5, 8, 1024), forces


def solution(mesh):
    in_specs = (
        P(None, None, ("freq", "space"), None),
        P(None, None, None, ("freq", "space"), None),
        P(None, ("freq", "space"), None),
        P(),
        P(),
        P("space"),
        P("space"),
        P("space", None),
    )
    out_specs = (P(None, None, ("freq", "space"), None), P(None, ("freq", "space")))
    return jax.shard_map(local, mesh=mesh, in_specs=in_specs, out_specs=out_specs, check_vma=False)
```

time: 181 us -> 92.5 us (0.51)
  starting transfers between devices: 102 us -> 9.56 us
  blocking collectives: 0 us -> 44.3 us
  Pallas kernels: 0 us -> 20.4 us
  local copies, waits for them, and re-layouts: 18.1 us -> 0.72 us
  other arithmetic: 15.4 us -> 0 us
  matrix products: 13.9 us -> 0 us
  waiting for transfers between devices: 30 us -> 16.4 us
    all_to_all x3 -> x0, starting transfers between devices: 52.7 us -> none  [the longest x1 27.3 us: local(): lax.all_to_all(local_index, 'space', split_axis=1, concat_axis=1, tiled=T...]
    all_to_all x0 -> x2, blocking collectives: none -> 44.3 us  [the longest x1 28.5 us: local(): lax.all_to_all(packet.reshape(64, 1, LANES), 'space', 0, 0, tiled=True)]
    ppermute x16 -> x4, starting transfers between devices: 49 us -> 9.56 us  [exchange(): return (lax.ppermute(high, 'space', up), lax.ppermute(low, 'space', down))]
    all_to_all x3 -> x0, waiting for transfers between devices: 23.7 us -> none  [the longest x1 12.2 us: local(): lax.all_to_all(outgoing, 'space', split_axis=1, concat_axis=1, tiled=True)]
    pallas_call x0 -> x7, Pallas kernels: none -> 20.4 us  [call(): pl.pallas_call(kernel, out_shape=[jax.ShapeDtypeStruct(shape, F32) for sh...]
    dot_general x17 -> x0, matrix products: 13.9 us -> none  [the longest x8 7.37 us: couple(): jnp.einsum('kj,rjpq->rkpq', flux_jac[1], along_cells, precision=lax.Preci...]
    ppermute x16 -> x4, waiting for transfers between devices: 6.25 us -> 16.4 us  [exchange(): return (lax.ppermute(high, 'space', up), lax.ppermute(low, 'space', down))]
    gather x4 -> x0, local copies, waits for them, and re-layouts: 8.19 us -> none  [the longest x1 3.49 us: local(): local_index = (jnp.take(interface_slot, ranking) % row_count)[None]]
  transfers between devices with their start and end apart: 19 -> 4, of which waited for: 7 -> 4; matrix products, arithmetic and copies ran while one was open for 10% -> 1% of each run, Pallas kernels for 0% -> 5%
where the time goes in v1:
time: 92.5 us; the launch traced here: 92.1 us
  blocking collectives  44.3 us (48%)
  Pallas kernels  20.4 us (22%)
  waiting for transfers between devices  16.4 us (18%)
  starting transfers between devices  9.56 us (10%)
    all_to_all x1, blocking collectives, local(): lax.all_to_all(packet.reshape(64, 1, LANES), 'space', 0, 0, tiled=True)  28.5 us
    pallas_call x7, Pallas kernels, call(): pl.pallas_call(kernel, out_shape=[jax.ShapeDtypeStruct(shape, F32) for sh...  20.4 us
    ppermute x4, waiting for transfers between devices, exchange(): return (lax.ppermute(high, 'space', up), lax.ppermute(low, 'space', down))  16.4 us
    all_to_all x1, blocking collectives, local(): lax.all_to_all(shares.reshape(64, 1, LANES), 'space', 0, 0, tiled=True)  15.8 us
    ppermute x4, starting transfers between devices, exchange(): return (lax.ppermute(high, 'space', up), lax.ppermute(low, 'space', down))  9.56 us
  transfers between devices with their start and end apart: 4, of which 4 were waited for; matrix products, arithmetic and copies ran while one was open for 1% of the time, Pallas kernels for 5%

profile of v1, /device:TPU:6, one launch (start us, length us, event | category | flops | bytes accessed | tf_op | source)
XLA Modules:
  0.0 92.1 jit_solution(4481072890875537567)
XLA Ops:
  0.6 1.6 %shard_map.95 = (f32[69,2,8,128]{3,2,1,0:T(8,128)S(1)}, f32[69,2,8,128]{3,2,1,0:T(8,128)S(1)}) custom-call(f32[10,8,1024]{2,1,0:T(8,128)} %bitcast.23, f32[50,8,1024]{2,1,0:T(8,128)} %bitcast.21, f32[4,8,1024]{2,1,0:T(8,128)} %face.3), custom_call_target="tpu_custom_call" | custom-call | flops 1000000 | bytes 1000 | tf_op jit(solution)/shard_map/pallas_call | solution.py:265
  2.2 3.5 %collective-permute-start = (f32[69,2,8,128]{3,2,1,0:T(8,128)S(1)}, f32[69,2,8,128]{3,2,1,0:T(8,128)S(1)}, u32[]{:S(2)}, u32[]{:S(2)}) collective-permute-start(f32[69,2,8,128]{3,2,1,0:T(8,128)S(1)} %get-tuple-element.17), channel_id=1, source_target_pairs={{0,1},{1,2},{2,3},{3,4},{4,5},{5,6},{6,7},{7,8},{8,9},{9,10},{10,1... | collective-permute-start | bytes 1695752 | tf_op jit(solution)/shard_map/ppermute | solution.py:285
  5.7 1.3 %collective-permute-start.1 = (f32[69,2,8,128]{3,2,1,0:T(8,128)S(1)}, f32[69,2,8,128]{3,2,1,0:T(8,128)S(1)}, u32[]{:S(2)}, u32[]{:S(2)}) collective-permute-start(f32[69,2,8,128]{3,2,1,0:T(8,128)S(1)} %get-tuple-element.18), channel_id=1, source_target_pairs={{1,0},{2,1},{3,2},{4,3},{5,4},{6,5},{7,6},{8,7},{9,8},{10,9},{11,1... | collective-permute-start | bytes 1695752 | tf_op jit(solution)/shard_map/ppermute | solution.py:285
  7.0 0.7 copy.18.flux
  7.7 4.2 %shard_map.96 = (f32[64,12,8,128]{3,2,1,0:T(8,128)S(1)}, f32[80,14,8,128]{3,2,1,0:T(8,128)S(1)}) custom-call(f32[2,5,5]{2,1,0:T(8,128)S(1)} %copy.18.flux, f32[10,8,1024]{2,1,0:T(8,128)} %bitcast.24, f32[50,8,1024]{2,1,0:T(8,128)} %bitcast.22, f32[4,8,1024]{2,1,0:T(8,128)} %face.3), custom_call_target="tpu_custom_call" | custom-call | flops 1000000 | bytes 1000 | tf_op jit(solution)/shard_map/pallas_call | solution.py:265
  11.9 0.0 copy-start.1
  11.9 0.0 copy-start.2
  11.9 0.0 copy-start.3
  11.9 5.8 %collective-permute-done.got_low = f32[69,2,8,128]{3,2,1,0:T(8,128)S(1)} collective-permute-done((f32[69,2,8,128]{3,2,1,0:T(8,128)S(1)}, f32[69,2,8,128]{3,2,1,0:T(8,128)S(1)}, u32[]{:S(2)}, u32[]{:S(2)}) %collective-permute-start) | collective-permute-done | bytes 565280 | tf_op jit(solution)/shard_map/ppermute | solution.py:285
  17.7 4.1 %collective-permute-done.1.got_high = f32[69,2,8,128]{3,2,1,0:T(8,128)S(1)} collective-permute-done((f32[69,2,8,128]{3,2,1,0:T(8,128)S(1)}, f32[69,2,8,128]{3,2,1,0:T(8,128)S(1)}, u32[]{:S(2)}, u32[]{:S(2)}) %collective-permute-start.1) | collective-permute-done | bytes 565280 | tf_op jit(solution)/shard_map/ppermute | solution.py:285
  21.9 5.2 %shard_map.97 = (f32[64,12,8,128]{3,2,1,0:T(8,128)S(1)}, f32[80,14,8,128]{3,2,1,0:T(8,128)S(1)}, f32[50,8,128]{2,1,0:T(8,128)S(1)}, f32[50,8,128]{2,1,0:T(8,128)S(1)}) custom-call(f32[2,5,5]{2,1,0:T(8,128)S(1)} %copy.18.flux, f32[69,2,8,128]{3,2,1,0:T(8,128)S(1)} %collective-permute-done.got_low, ...), custom_call_target="tpu_custom_call", output_to_operand_aliasing={{0}: (3, {}), {1}: (4, {})} | custom-call | flops 1000000 | bytes 1000 | tf_op jit(solution)/shard_map/pallas_call | solution.py:265
  27.1 3.5 %collective-permute-start.2 = (f32[50,8,128]{2,1,0:T(8,128)S(1)}, f32[50,8,128]{2,1,0:T(8,128)S(1)}, u32[]{:S(2)}, u32[]{:S(2)}) collective-permute-start(f32[50,8,128]{2,1,0:T(8,128)S(1)} %get-tuple-element.21), channel_id=1, source_target_pairs={{0,1},{1,2},{2,3},{3,4},{4,5},{5,6},{6,7},{7,8},{8,9},{9,10},{10,1... | collective-permute-start | bytes 614408 | tf_op jit(solution)/shard_map/ppermute | solution.py:285
  30.6 1.3 %collective-permute-start.3 = (f32[50,8,128]{2,1,0:T(8,128)S(1)}, f32[50,8,128]{2,1,0:T(8,128)S(1)}, u32[]{:S(2)}, u32[]{:S(2)}) collective-permute-start(f32[50,8,128]{2,1,0:T(8,128)S(1)} %get-tuple-element.22), channel_id=1, source_target_pairs={{1,0},{2,1},{3,2},{4,3},{5,4},{6,5},{7,6},{8,7},{9,8},{10,9},{11,1... | collective-permute-start | bytes 614408 | tf_op jit(solution)/shard_map/ppermute | solution.py:285
  31.9 0.0 copy-done.1
  31.9 0.0 copy-done.2
  31.9 0.7 shard_map.98
  32.6 1.2 %collective-permute-done.2.got_low = f32[50,8,128]{2,1,0:T(8,128)S(1)} collective-permute-done((f32[50,8,128]{2,1,0:T(8,128)S(1)}, f32[50,8,128]{2,1,0:T(8,128)S(1)}, u32[]{:S(2)}, u32[]{:S(2)}) %collective-permute-start.2) | collective-permute-done | bytes 204832 | tf_op jit(solution)/shard_map/ppermute | solution.py:285
  33.9 5.2 %collective-permute-done.3.got_high = f32[50,8,128]{2,1,0:T(8,128)S(1)} collective-permute-done((f32[50,8,128]{2,1,0:T(8,128)S(1)}, f32[50,8,128]{2,1,0:T(8,128)S(1)}, u32[]{:S(2)}, u32[]{:S(2)}) %collective-permute-start.3) | collective-permute-done | bytes 204832 | tf_op jit(solution)/shard_map/ppermute | solution.py:285
  39.1 0.0 copy-done.3
  39.1 0.0 copy-start
  39.1 6.9 %shard_map.99 = (f32[80,14,8,128]{3,2,1,0:T(8,128)S(1)}, f32[10,8,1024]{2,1,0:T(8,128)}, f32[64,128]{1,0:T(8,128)S(1)}) custom-call(f32[2,5,5]{2,1,0:T(8,128)S(1)} %copy.18.flux, f32[5]{0:T(128)S(1)} %copy-done.3, f32[50,8,128]{2,1,0:T(8,128)S(1)} %collective-permute-done.2.got_low, ...), custom_call_target="tpu_custom_call", output_to_operand_aliasing={{0}: (5, {})} | custom-call | flops 1000000 | bytes 1000 | tf_op jit(solution)/shard_map/pallas_call | solution.py:265
  46.0 28.5 %all_to_all.10 = f32[64,1,128]{2,1,0:T(1,128)S(1)} all-to-all(f32[64,1,128]{2,1,0:T(1,128)S(1)} %bitcast.18), channel_id=1, replica_groups=mesh['freq'=8,'space'=64] {'space'}, dimensions={0} | all-to-all | bytes 65536 | tf_op jit(solution)/shard_map/all_to_all | solution.py:329
  74.4 0.0 copy-done
  74.4 1.2 %shard_map.100 = f32[64,128]{1,0:T(8,128)S(1)} custom-call(f32[64,128]{1,0:T(8,128)S(1)} %bitcast.15, f32[192,512]{1,0:T(8,128)S(1)} %bitcast.14), custom_call_target="tpu_custom_call" | custom-call | flops 1000000 | bytes 1000 | tf_op jit(solution)/shard_map/pallas_call | solution.py:265
  75.6 15.8 %all_to_all.11 = f32[64,1,128]{2,1,0:T(1,128)S(1)} all-to-all(f32[64,1,128]{2,1,0:T(1,128)S(1)} %bitcast.16), channel_id=1, replica_groups=mesh['freq'=8,'space'=64] {'space'}, dimensions={0} | all-to-all | bytes 65536 | tf_op jit(solution)/shard_map/all_to_all | solution.py:331
  91.5 0.6 shard_map.101
Async XLA Ops:
  2.2 15.5 %collective-permute-start = (f32[69,2,8,128]{3,2,1,0:T(8,128)S(1)}, f32[69,2,8,128]{3,2,1,0:T(8,128)S(1)}, u32[]{:S(2)}, u32[]{:S(2)}) collective-permute-start(f32[69,2,8,128]{3,2,1,0:T(8,128)S(1)} %get-tuple-element.17), channel_id=1, source_target_pairs={{0,1},{1,2},{2,3},{3,4},{4,5},{5,6},{6,7},{7,8},{8,9},{9,10},{10,1... | collective-permute-start | bytes 1695752 | tf_op jit(solution)/shard_map/ppermute | solution.py:285
  5.7 16.2 %collective-permute-start.1 = (f32[69,2,8,128]{3,2,1,0:T(8,128)S(1)}, f32[69,2,8,128]{3,2,1,0:T(8,128)S(1)}, u32[]{:S(2)}, u32[]{:S(2)}) collective-permute-start(f32[69,2,8,128]{3,2,1,0:T(8,128)S(1)} %get-tuple-element.18), channel_id=1, source_target_pairs={{1,0},{2,1},{3,2},{4,3},{5,4},{6,5},{7,6},{8,7},{9,8},{10,9},{11,1... | collective-permute-start | bytes 1695752 | tf_op jit(solution)/shard_map/ppermute | solution.py:285
  11.9 20.0 %copy-start.1 = (s32[512]{0:T(512)S(1)}, s32[512]{0:T(512)}, u32[]{:S(2)}) copy-start(s32[512]{0:T(512)} %param.14) | copy-start | bytes 6148
  11.9 20.0 %copy-start.2 = (s32[512]{0:T(512)S(1)}, s32[512]{0:T(512)}, u32[]{:S(2)}) copy-start(s32[512]{0:T(512)} %param.13) | copy-start | bytes 6148
  11.9 27.1 %copy-start.3 = (f32[5]{0:T(128)S(1)}, f32[5]{0:T(128)}, u32[]{:S(2)}) copy-start(f32[5]{0:T(128)} %weights.1) | copy-start | bytes 64
  27.1 6.7 %collective-permute-start.2 = (f32[50,8,128]{2,1,0:T(8,128)S(1)}, f32[50,8,128]{2,1,0:T(8,128)S(1)}, u32[]{:S(2)}, u32[]{:S(2)}) collective-permute-start(f32[50,8,128]{2,1,0:T(8,128)S(1)} %get-tuple-element.21), channel_id=1, source_target_pairs={{0,1},{1,2},{2,3},{3,4},{4,5},{5,6},{6,7},{7,8},{8,9},{9,10},{10,1... | collective-permute-start | bytes 614408 | tf_op jit(solution)/shard_map/ppermute | solution.py:285
  30.6 8.5 %collective-permute-start.3 = (f32[50,8,128]{2,1,0:T(8,128)S(1)}, f32[50,8,128]{2,1,0:T(8,128)S(1)}, u32[]{:S(2)}, u32[]{:S(2)}) collective-permute-start(f32[50,8,128]{2,1,0:T(8,128)S(1)} %get-tuple-element.22), channel_id=1, source_target_pairs={{1,0},{2,1},{3,2},{4,3},{5,4},{6,5},{7,6},{8,7},{9,8},{10,9},{11,1... | collective-permute-start | bytes 614408 | tf_op jit(solution)/shard_map/ppermute | solution.py:285
  39.1 35.4 %copy-start = (f32[512,192]{0,1:T(8,128)S(1)}, f32[512,192]{0,1:T(8,128)}, u32[]{:S(2)}) copy-start(f32[512,192]{0,1:T(8,128)} %param.15) | copy-start | bytes 1179652

commit v2 on v1

v2 whole, which is shorter than its diff:
```python
import jax
import jax.numpy as jnp
from jax import lax
from jax.experimental import pallas as pl
from jax.experimental.pallas import tpu as pltpu
from jax.sharding import PartitionSpec as P


INTERPRET = False
HI = lax.Precision.HIGHEST
F32 = jnp.float32
RHS = 50
FAC = 60
NF = 64
LANES = 128
MIB = 1 << 20


def tile_iota(dim):
    return lax.broadcasted_iota(jnp.int32, (8, LANES), dim)


def matvec(blk, vec):
    out = []
    for r in range(2):
        for k in range(5):
            acc = None
            for j in range(5):
                br, bi = blk(k * 5 + j), blk(25 + k * 5 + j)
                if r == 0:
                    term = br * vec[j] - bi * vec[5 + j]
                else:
                    term = br * vec[5 + j] + bi * vec[j]
                acc = term if acc is None else acc + term
            out.append(acc)
    return out


def next_cell(x):
    rolled = pltpu.roll(x, LANES - 1, 1)
    return jnp.where(tile_iota(1) == LANES - 1, pltpu.roll(rolled, 7, 0), rolled)


def prev_cell(x):
    rolled = pltpu.roll(x, 1, 1)
    return jnp.where(tile_iota(1) == 0, pltpu.roll(rolled, 1, 0), rolled)


def start_state(cx, st, planes):
    for plane in planes:
        c, e = plane + 2, plane + 3
        new = matvec(lambda f: cx[f, c], [cx[RHS + f, c] for f in range(10)])
        for f in range(10):
            st[f, e] = new[f]


def advance(cx, st, flux, level, planes, out=None):
    base = (level - 1) * 10
    last = (tile_iota(0) == 7) & (tile_iota(1) == LANES - 1)
    first = (tile_iota(0) == 0) & (tile_iota(1) == 0)
    for plane in planes:
        c, e = plane + 2, plane + 3
        f0, f1, f2, f3 = [cx[FAC + n, c] for n in range(4)]
        f2 = jnp.where(last, 0.0, f2)
        f3 = jnp.where(first, 0.0, f3)
        vec = []
        for r in range(2):
            across, along = [], []
            for j in range(5):
                n = base + r * 5 + j
                here = st[n, e]
                across.append(f0 * st[n, e + 1] + f1 * st[n, e - 1])
                along.append(f2 * next_cell(here) + f3 * prev_cell(here))
            for k in range(5):
                acc = cx[RHS + r * 5 + k, c]
                for j in range(5):
                    acc = acc + flux[0, k, j] * across[j]
                for j in range(5):
                    acc = acc + flux[1, k, j] * along[j]
                vec.append(acc)
        new = matvec(lambda f: cx[f, c], vec)
        for f in range(10):
            if out is None:
                st[level * 10 + f, e] = new[f]
            else:
                out[f, plane] = new[f]


def run(low, high, body):
    if low == high:
        body((low, 7 - low))
    else:

        @pl.loop(low, high + 1)
        def _(plane):
            body((plane, 7 - plane))


def plane_copies(source, target, sems, first, count, offset, at):
    copies = []
    for j in range(8):
        copies.append(
            pltpu.make_async_copy(
                source.at[:, first : first + count, j * LANES : (j + 1) * LANES],
                target.at[offset : offset + source.shape[0], at : at + count, j, :],
                sems,
            )
        )
    return copies


def pack_kernel(rhs, inv, face, low, high, edge, sems):
    copies = []
    for side, (target, first, inner) in enumerate(((low, 0, 2), (high, 6, 5))):
        copies += plane_copies(inv, target, sems.at[side], first, 2, 0, 0)
        copies += plane_copies(rhs, target, sems.at[side], first, 2, RHS, 0)
        copies += plane_copies(face, target, sems.at[side], first, 2, FAC, 0)
        copies += plane_copies(inv, edge, sems.at[side], inner, 1, 0, side)
        copies += plane_copies(rhs, edge, sems.at[side], inner, 1, RHS, side)
    for copy in copies:
        copy.start()
    for copy in copies:
        copy.wait()
    for side, target in enumerate((low, high)):
        new = matvec(lambda f: edge[f, side], [edge[RHS + f, side] for f in range(10)])
        for f in range(10):
            target[NF + f // 2, f % 2] = new[f]


def inner_kernel(flux, rhs, inv, face, cx, st, sems):
    copies = (
        plane_copies(inv, cx, sems.at[0], 0, 8, 0, 2)
        + plane_copies(rhs, cx, sems.at[0], 0, 8, RHS, 2)
        + plane_copies(face, cx, sems.at[0], 0, 8, FAC, 2)
    )
    for copy in copies:
        copy.start()
    for copy in copies:
        copy.wait()
    run(0, 3, lambda p: start_state(cx, st, p))
    for level in (1, 2, 3):
        run(level, 3, lambda p: advance(cx, st, flux, level, p))


def middle_kernel(flux, got_low, got_high, cx_in, st_in, cx, st, low, high, mid):
    del cx_in, st_in
    @pl.loop(0, NF)
    def _(f):
        for p in range(2):
            cx[f, p] = got_low[f, p]
            cx[f, 10 + p] = got_high[f, p]

    for f in range(10):
        st[f, 0] = got_low[NF + f // 2, f % 2]
        st[f, 13] = got_high[NF + f // 2, f % 2]
    run(-2, -1, lambda p: start_state(cx, st, p))
    for level in (1, 2, 3):
        run(level - 3, level - 1, lambda p: advance(cx, st, flux, level, p))
    run(1, 3, lambda p: advance(cx, st, flux, 4, p))
    run(2, 3, lambda p: advance(cx, st, flux, 5, p))
    run(3, 3, lambda p: advance(cx, st, flux, 6, p))
    for n, (level, low_plane, high_plane) in enumerate(EDGES):
        for f in range(10):
            low[n * 10 + f] = st[level * 10 + f, low_plane + 3]
            high[n * 10 + f] = st[level * 10 + f, high_plane + 3]
    for n, (level, plane) in enumerate(MIDDLE):
        for f in range(10):
            mid[n * 10 + f] = st[level * 10 + f, plane + 3]


EDGES = ((3, 0, 6), (3, 1, 7), (4, 1, 5), (4, 2, 6), (5, 2, 5))
MIDDLE = ((5, 3), (5, 4), (6, 3), (6, 4))


def last_kernel(
    flux, weights, got_low, got_high, low, high, mid, cx, ordered, out, value, st, final, sems
):
    for n, (level, low_plane, high_plane) in enumerate(EDGES):
        for f in range(10):
            at = (level - 3) * 10 + f
            st[at, low_plane + 8 + 3] = got_high[n * 10 + f]
            st[at, high_plane - 8 + 3] = got_low[n * 10 + f]
            st[at, low_plane + 3] = low[n * 10 + f]
            st[at, high_plane + 3] = high[n * 10 + f]
    for n, (level, plane) in enumerate(MIDDLE):
        for f in range(10):
            st[(level - 3) * 10 + f, plane + 3] = mid[n * 10 + f]
    run(-1, 0, lambda p: advance(cx, st, flux, 1, p))
    run(-2, 1, lambda p: advance(cx, st, flux, 2, p))
    run(-2, 2, lambda p: advance(cx, st, flux, 3, p))
    run(-1, 3, lambda p: advance(cx, st, flux, 4, p))
    run(0, 3, lambda p: advance(cx, st, flux, 5, p, out=final))
    copies = [
        pltpu.make_async_copy(final.at[:, :, j, :], out.at[:, :, j * LANES : (j + 1) * LANES], sems.at[0])
        for j in range(8)
    ]
    for copy in copies:
        copy.start()
    press = []
    for r in range(2):
        acc = None
        for j in range(5):
            term = weights[j] * final[r * 5 + j].reshape(64, LANES)
            acc = term if acc is None else acc + term
        press.append(acc)
    cells = as_column(ordered[0:1, :])
    lane = lax.broadcasted_iota(jnp.int32, cells.shape, 1)
    rows = jnp.where(lane == cells // LANES, 1.0, 0.0)[:, 0:64]
    column = []
    for r in range(2):
        picked = jnp.dot(rows, press[r], precision=HI, preferred_element_type=F32)
        column.append(jnp.sum(jnp.where(lane == cells % LANES, picked, 0.0), axis=1, keepdims=True))
    value[...] = jnp.where(lane == 0, column[0], column[1]).T[0:8, :]
    for copy in copies:
        copy.wait()


def as_column(row):
    return jnp.broadcast_to(row.astype(F32), (LANES, row.shape[1])).T.astype(jnp.int32)


def route_kernel(slot_row, cell_row, ordered, wanted):
    slots, cells = slot_row[...], cell_row[...]
    rows = slots.shape[1]
    owners = wanted.shape[0]
    share = rows // owners
    owner = slots // rows
    local = (slots - owner * rows).astype(F32)
    below = lax.broadcasted_iota(jnp.int32, (rows, rows), 0)
    across = lax.broadcasted_iota(jnp.int32, (rows, rows), 1)
    earlier = jnp.where((as_column(owner)[:, 0:1] == owner) & (below < across), 1.0, 0.0)
    place = jnp.sum(earlier, axis=0, keepdims=True).astype(jnp.int32)
    move = jnp.where(owner * share + place == below, cells.astype(F32), 0.0)
    move = jnp.sum(move, axis=1, keepdims=True)
    ordered[...] = jnp.broadcast_to(move, (rows, LANES)).T[0:8, :]
    by_owner = jnp.where(lax.broadcasted_iota(jnp.int32, (owners, rows), 0) == owner, 1.0, 0.0)
    by_place = jnp.where(lax.broadcasted_iota(jnp.int32, (8, rows), 0) == place, local, 0.0)
    wanted[...] = jnp.zeros(wanted.shape, F32)
    wanted[:, 0:8] = lax.dot_general(
        by_owner, by_place, (((1,), (1,)), ((), ())), precision=HI, preferred_element_type=F32
    )


def gather_kernel(asked, modes_t, rows_out):
    count = modes_t.shape[1]
    modes_n = modes_t.shape[0]
    places = lax.broadcasted_iota(jnp.int32, (64, count), 1)
    got = asked[...]
    rows_out[...] = jnp.zeros(rows_out.shape, F32)
    for i in range(8):
        hit = jnp.where(got[:, i : i + 1].astype(jnp.int32) == places, 1.0, 0.0)
        rows_out[:, i, 0:modes_n] = lax.dot_general(
            hit, modes_t[...], (((1,), (1,)), ((), ())), precision=HI, preferred_element_type=F32
        )


def force_kernel(value, rows_in, shares):
    rows = rows_in[...].reshape(512, 256)
    total = []
    column = value[...].T
    for r in range(2):
        total.append(jnp.sum(rows * column[:, r : r + 1], axis=0, keepdims=True))
    line = lax.broadcasted_iota(jnp.int32, (8, 256), 0)
    mode = lax.broadcasted_iota(jnp.int32, (8, 256), 1)
    kept = jnp.where((mode % 3 == line % 3) & (line < 6), jnp.where(line < 3, total[0], total[1]), 0.0)
    mine = lax.broadcasted_iota(jnp.int32, (64, 256), 1) // 3 == lax.broadcasted_iota(jnp.int32, (64, 256), 0)
    shares[...] = jnp.zeros(shares.shape, F32)
    shares[:, 0:8] = lax.dot_general(
        jnp.where(mine, 1.0, 0.0), kept, (((1,), (1,)), ((), ())), precision=HI, preferred_element_type=F32
    )


def total_kernel(arrived, forces):
    total = jnp.sum(arrived[...], axis=0, keepdims=True)
    forces[0:1, :] = total[:, 0:3]
    forces[1:2, :] = total[:, 3:6]


def call(kernel, outs, ins, scratch=(), aliases=None, cost=None, vmem=24 * MIB):
    return pl.pallas_call(
        kernel,
        out_shape=[jax.ShapeDtypeStruct(shape, F32) for shape, _ in outs],
        in_specs=[pl.BlockSpec(memory_space=space) for _, space in ins],
        out_specs=[pl.BlockSpec(memory_space=space) for _, space in outs],
        scratch_shapes=list(scratch),
        input_output_aliases=aliases or {},
        compiler_params=pltpu.CompilerParams(vmem_limit_bytes=vmem),
        cost_estimate=pl.CostEstimate(flops=cost or 1000000, bytes_accessed=1000, transcendentals=0),
        interpret=INTERPRET,
    )(*[array for array, _ in ins])


V, S, A = pltpu.VMEM, pltpu.SMEM, pl.ANY


def exchange(low, high):
    count = lax.axis_size("space")
    up = [(i, i + 1) for i in range(count - 1)]
    down = [(target, source) for source, target in up]
    return lax.ppermute(high, "space", up), lax.ppermute(low, "space", down)


def trade(parts):
    return lax.all_to_all(parts, "space", 0, 0, tiled=True)


def program(rhs, inv_diag, face_coef, flux_jac, press_weights, surface_cells, interface_slot, mode_shapes):
    rhs_f = pltpu.with_memory_space_constraint(rhs.reshape(10, 8, 1024), pltpu.HBM)
    inv_f = pltpu.with_memory_space_constraint(inv_diag.reshape(50, 8, 1024), pltpu.HBM)
    face_coef = pltpu.with_memory_space_constraint(face_coef, pltpu.HBM)
    flux = flux_jac
    rows = interface_slot.shape[0]
    dma = pltpu.SemaphoreType.DMA

    low, high = call(
        pack_kernel,
        [((NF + 5, 2, 8, LANES), V)] * 2,
        [(rhs_f, A), (inv_f, A), (face_coef, A)],
        [pltpu.VMEM((60, 2, 8, LANES), F32), dma((2,))],
    )
    got_low, got_high = exchange(low, high)

    ordered, wanted = call(
        route_kernel,
        [((8, rows), V), ((64, LANES), V)],
        [(interface_slot.reshape(1, rows), V), (surface_cells.reshape(1, rows), V)],
    )
    asked = trade(wanted.reshape(64, 1, LANES)).reshape(64, LANES)
    cx, st = call(
        inner_kernel,
        [((NF, 12, 8, LANES), V), ((70, 14, 8, LANES), V)],
        [(flux, S), (rhs_f, A), (inv_f, A), (face_coef, A)],
        [dma((1,))],
    )
    cx, st, low, high, mid = call(
        middle_kernel,
        [((NF, 12, 8, LANES), V), ((70, 14, 8, LANES), V), ((50, 8, LANES), V), ((50, 8, LANES), V), ((40, 8, LANES), V)],
        [(flux, S), (got_low, V), (got_high, V), (cx, V), (st, V)],
        aliases={3: 0, 4: 1},
    )
    got_low, got_high = exchange(low, high)
    (mode_rows,) = call(gather_kernel, [((64, 8, 256), V)], [(asked, V), (mode_shapes.T, V)])
    mode_rows = trade(mode_rows)
    state, value = call(
        last_kernel,
        [((10, 8, 1024), A), ((8, rows), V)],
        [(flux, S), (press_weights, S), (got_low, V), (got_high, V), (low, V), (high, V), (mid, V), (cx, V), (ordered, V)],
        [pltpu.VMEM((50, 14, 8, LANES), F32), pltpu.VMEM((10, 8, 8, LANES), F32), dma((1,))],
    )
    (shares,) = call(force_kernel, [((64, LANES), V)], [(value, V), (mode_rows, V)])
    arrived = trade(shares.reshape(64, 1, LANES))
    (forces,) = call(total_kernel, [((2, 3), V)], [(arrived.reshape(64, LANES), V)])
    return state.reshape(2, 5, 8, 1024), forces


def solution(mesh):
    in_specs = (
        P(None, None, ("freq", "space"), None),
        P(None, None, None, ("freq", "space"), None),
        P(None, ("freq", "space"), None),
        P(),
        P(),
        P("space"),
        P("space"),
        P("space", None),
    )
    out_specs = (P(None, None, ("freq", "space"), None), P(None, ("freq", "space")))
    return jax.shard_map(program, mesh=mesh, in_specs=in_specs, out_specs=out_specs, check_vma=False)
```

time: 92.5 us -> 115 us (1.24)
  blocking collectives: 44.3 us -> 54 us
  starting transfers between devices: 9.56 us -> 14 us
  waiting for transfers between devices: 16.4 us -> 19.6 us
  Pallas kernels: 20.4 us -> 23.4 us
  local copies, waits for them, and re-layouts: 0.72 us -> 2.36 us
    all_to_all x2, blocking collectives: 44.3 us -> 54 us  [trade(): return lax.all_to_all(parts, 'space', 0, 0, tiled=True)]
    all_to_all x0 -> x1, starting transfers between devices: none -> 4.63 us  [trade(): return lax.all_to_all(parts, 'space', 0, 0, tiled=True)]
    ppermute x4, waiting for transfers between devices: 16.4 us -> 19.6 us  [exchange(): return (lax.ppermute(high, 'space', up), lax.ppermute(low, 'space', down))]
    pallas_call x7 -> x8, Pallas kernels: 20.4 us -> 23.4 us  [call(): pl.pallas_call(kernel, out_shape=[jax.ShapeDtypeStruct(shape, F32) for sh...]
    unnamed x9 -> x11, local copies, waits for them, and re-layouts: 0.72 us -> 2.36 us
  transfers between devices with their start and end apart: 4 -> 5, of which waited for: 4 -> 4; matrix products, arithmetic and copies ran while one was open for 1% -> 0% of each run, Pallas kernels for 5% -> 15%
where the time goes in v2:
time: 115 us; the launch traced here: 114 us
  blocking collectives  54 us (47%)
  Pallas kernels  23.4 us (20%)
  waiting for transfers between devices  19.6 us (17%)
  starting transfers between devices  14 us (12%)
  local copies, waits for them, and re-layouts  2.36 us (2%)
    all_to_all x2, blocking collectives, trade(): return lax.all_to_all(parts, 'space', 0, 0, tiled=True)  54 us
    pallas_call x8, Pallas kernels, call(): pl.pallas_call(kernel, out_shape=[jax.ShapeDtypeStruct(shape, F32) for sh...  23.4 us
    ppermute x4, waiting for transfers between devices, exchange(): return (lax.ppermute(high, 'space', up), lax.ppermute(low, 'space', down))  19.6 us
    ppermute x4, starting transfers between devices, exchange(): return (lax.ppermute(high, 'space', up), lax.ppermute(low, 'space', down))  9.37 us
    all_to_all x1, starting transfers between devices, trade(): return lax.all_to_all(parts, 'space', 0, 0, tiled=True)  4.63 us
    unnamed x11, local copies, waits for them, and re-layouts  2.36 us
  transfers between devices with their start and end apart: 5, of which 4 were waited for; matrix products, arithmetic and copies ran while one was open for 0% of the time, Pallas kernels for 15%

profile of v2, /device:TPU:6, one launch (start us, length us, event | category | flops | bytes accessed | tf_op | source)
XLA Modules:
  0.0 114.1 jit_solution(1350888128015296164)
XLA Ops:
  0.6 0.0 copy-start.1
  0.6 0.7 copy-done.1
  1.3 0.0 copy-start.2
  1.3 0.7 copy-done.2
  2.0 0.0 copy-start.4
  2.0 0.6 shard_map.98
  2.6 28.4 %all_to_all.15 = f32[64,1,128]{2,1,0:T(1,128)S(1)} all-to-all(f32[64,1,128]{2,1,0:T(1,128)S(1)} %bitcast.18), channel_id=1, replica_groups=mesh['freq'=8,'space'=64] {'space'}, dimensions={0} | all-to-all | bytes 65536 | tf_op jit(solution)/shard_map/all_to_all | solution.py:304
  31.0 0.0 copy-start
  31.0 1.0 copy-done
  32.0 4.0 %shard_map.100 = f32[64,8,256]{2,1,0:T(8,128)} custom-call(f32[64,128]{1,0:T(8,128)S(1)} %bitcast.17, f32[192,512]{1,0:T(8,128)S(1)} %bitcast.14), custom_call_target="tpu_custom_call" | custom-call | flops 1000000 | bytes 1000 | tf_op jit(solution)/shard_map/pallas_call | solution.py:280
  36.0 4.6 %all-to-all-start.1 = ((f32[64,8,256]{2,1,0:T(8,128)}), f32[64,8,256]{2,1,0:T(8,128)S(1)}, u32[]{:S(2)}, u32[]{:S(2)}) async-start(f32[64,8,256]{2,1,0:T(8,128)} %shard_map.100), calls=%async_computation.1 | async-start | bytes 1048576 | tf_op jit(solution)/shard_map/all_to_all | solution.py:304
  40.6 1.6 %shard_map.95 = (f32[69,2,8,128]{3,2,1,0:T(8,128)S(1)}, f32[69,2,8,128]{3,2,1,0:T(8,128)S(1)}) custom-call(f32[10,8,1024]{2,1,0:T(8,128)} %bitcast.23, f32[50,8,1024]{2,1,0:T(8,128)} %bitcast.21, f32[4,8,1024]{2,1,0:T(8,128)} %face.3), custom_call_target="tpu_custom_call" | custom-call | flops 1000000 | bytes 1000 | tf_op jit(solution)/shard_map/pallas_call | solution.py:280
  42.2 3.4 %collective-permute-start = (f32[69,2,8,128]{3,2,1,0:T(8,128)S(1)}, f32[69,2,8,128]{3,2,1,0:T(8,128)S(1)}, u32[]{:S(2)}, u32[]{:S(2)}) collective-permute-start(f32[69,2,8,128]{3,2,1,0:T(8,128)S(1)} %get-tuple-element.14), channel_id=1, source_target_pairs={{0,1},{1,2},{2,3},{3,4},{4,5},{5,6},{6,7},{7,8},{8,9},{9,10},{10,1... | collective-permute-start | bytes 1695752 | tf_op jit(solution)/shard_map/ppermute | solution.py:300
  45.6 1.3 %collective-permute-start.1 = (f32[69,2,8,128]{3,2,1,0:T(8,128)S(1)}, f32[69,2,8,128]{3,2,1,0:T(8,128)S(1)}, u32[]{:S(2)}, u32[]{:S(2)}) collective-permute-start(f32[69,2,8,128]{3,2,1,0:T(8,128)S(1)} %get-tuple-element.15), channel_id=1, source_target_pairs={{1,0},{2,1},{3,2},{4,3},{5,4},{6,5},{7,6},{8,7},{9,8},{10,9},{11,1... | collective-permute-start | bytes 1695752 | tf_op jit(solution)/shard_map/ppermute | solution.py:300
  46.9 0.0 copy-done.4
  46.9 4.1 %shard_map.96 = (f32[64,12,8,128]{3,2,1,0:T(8,128)S(1)}, f32[70,14,8,128]{3,2,1,0:T(8,128)S(1)}) custom-call(f32[2,5,5]{2,1,0:T(8,128)S(1)} %copy.17.flux, f32[10,8,1024]{2,1,0:T(8,128)} %bitcast.24, f32[50,8,1024]{2,1,0:T(8,128)} %bitcast.22, f32[4,8,1024]{2,1,0:T(8,128)} %face.3), custom_call_target="tpu_custom_call" | custom-call | flops 1000000 | bytes 1000 | tf_op jit(solution)/shard_map/pallas_call | solution.py:280
  51.0 11.5 %collective-permute-done.got_low = f32[69,2,8,128]{3,2,1,0:T(8,128)S(1)} collective-permute-done((f32[69,2,8,128]{3,2,1,0:T(8,128)S(1)}, f32[69,2,8,128]{3,2,1,0:T(8,128)S(1)}, u32[]{:S(2)}, u32[]{:S(2)}) %collective-permute-start) | collective-permute-done | bytes 565280 | tf_op jit(solution)/shard_map/ppermute | solution.py:300
  62.5 1.7 %collective-permute-done.1.got_high = f32[69,2,8,128]{3,2,1,0:T(8,128)S(1)} collective-permute-done((f32[69,2,8,128]{3,2,1,0:T(8,128)S(1)}, f32[69,2,8,128]{3,2,1,0:T(8,128)S(1)}, u32[]{:S(2)}, u32[]{:S(2)}) %collective-permute-start.1) | collective-permute-done | bytes 565280 | tf_op jit(solution)/shard_map/ppermute | solution.py:300
  64.2 0.0 copy-start.3
  64.2 5.2 %shard_map.97 = (f32[64,12,8,128]{3,2,1,0:T(8,128)S(1)}, f32[70,14,8,128]{3,2,1,0:T(8,128)S(1)}, f32[50,8,128]{2,1,0:T(8,128)S(1)}, f32[50,8,128]{2,1,0:T(8,128)S(1)}, f32[40,8,128]{2,1,0:T(8,128)S(1)}) custom-call(f32[2,5,5]{2,1,0:T(8,128)S(1)} %copy.17.flux, ...), custom_call_target="tpu_custom_call", output_to_operand_aliasing={{0}: (3, {}), {1}: (4, {})} | custom-call | flops 1000000 | bytes 1000 | tf_op jit(solution)/shard_map/pallas_call | solution.py:280
  69.5 3.4 %collective-permute-start.2 = (f32[50,8,128]{2,1,0:T(8,128)S(1)}, f32[50,8,128]{2,1,0:T(8,128)S(1)}, u32[]{:S(2)}, u32[]{:S(2)}) collective-permute-start(f32[50,8,128]{2,1,0:T(8,128)S(1)} %get-tuple-element.18.high), channel_id=1, source_target_pairs={{0,1},{1,2},{2,3},{3,4},{4,5},{5,6},{6,7},{7,8},{8,9},{9,10},{10,1... | collective-permute-start | bytes 614408 | tf_op jit(solution)/shard_map/ppermute | solution.py:300
  72.8 1.3 %collective-permute-start.3 = (f32[50,8,128]{2,1,0:T(8,128)S(1)}, f32[50,8,128]{2,1,0:T(8,128)S(1)}, u32[]{:S(2)}, u32[]{:S(2)}) collective-permute-start(f32[50,8,128]{2,1,0:T(8,128)S(1)} %get-tuple-element.19.low), channel_id=1, source_target_pairs={{1,0},{2,1},{3,2},{4,3},{5,4},{6,5},{7,6},{8,7},{9,8},{10,9},{11,1... | collective-permute-start | bytes 614408 | tf_op jit(solution)/shard_map/ppermute | solution.py:300
  74.1 2.0 %collective-permute-done.2.got_low = f32[50,8,128]{2,1,0:T(8,128)S(1)} collective-permute-done((f32[50,8,128]{2,1,0:T(8,128)S(1)}, f32[50,8,128]{2,1,0:T(8,128)S(1)}, u32[]{:S(2)}, u32[]{:S(2)}) %collective-permute-start.2) | collective-permute-done | bytes 204832 | tf_op jit(solution)/shard_map/ppermute | solution.py:300
  76.1 4.4 %collective-permute-done.3.got_high = f32[50,8,128]{2,1,0:T(8,128)S(1)} collective-permute-done((f32[50,8,128]{2,1,0:T(8,128)S(1)}, f32[50,8,128]{2,1,0:T(8,128)S(1)}, u32[]{:S(2)}, u32[]{:S(2)}) %collective-permute-start.3) | collective-permute-done | bytes 204832 | tf_op jit(solution)/shard_map/ppermute | solution.py:300
  80.5 0.0 copy-done.3
  80.5 6.8 %shard_map.99 = (f32[10,8,1024]{2,1,0:T(8,128)}, f32[8,512]{1,0:T(8,128)S(1)}) custom-call(f32[2,5,5]{2,1,0:T(8,128)S(1)} %copy.17.flux, f32[5]{0:T(128)S(1)} %copy-done.3, f32[50,8,128]{2,1,0:T(8,128)S(1)} %collective-permute-done.2.got_low, f32[50,8,128]{2,1,0:T(8,128)S(1)} %collective-permute-done.3.got_high, f32[50,8,128]{2,1,0:T(8,128)S(1)} %get-tuple-element.19.low, ...), custom_call_target="tpu_custom_call" | custom-call | flops 1000000 | bytes 1000 | tf_op jit(solution)/shard_map/pallas_call | solution.py:280
  87.3 0.0 all-to-all-done.1.rows_in
  87.3 0.6 shard_map.101
  87.9 25.6 %all_to_all.16 = f32[64,1,128]{2,1,0:T(1,128)S(1)} all-to-all(f32[64,1,128]{2,1,0:T(1,128)S(1)} %bitcast.15), channel_id=1, replica_groups=mesh['freq'=8,'space'=64] {'space'}, dimensions={0} | all-to-all | bytes 65536 | tf_op jit(solution)/shard_map/all_to_all | solution.py:304
  113.5 0.6 shard_map.102
  (1 shorter events, 0.0 us)
Async XLA Ops:
  0.6 0.7 copy-start.1
  1.3 0.7 copy-start.2
  2.0 44.9 %copy-start.4 = (f32[2,5,5]{2,0,1:T(2,128)S(1)}, f32[2,5,5]{2,0,1:T(2,128)}, u32[]{:S(2)}) copy-start(f32[2,5,5]{2,0,1:T(2,128)} %param.11) | copy-start | bytes 604
  31.0 1.0 copy-start
  36.0 51.4 %all-to-all-start.1 = ((f32[64,8,256]{2,1,0:T(8,128)}), f32[64,8,256]{2,1,0:T(8,128)S(1)}, u32[]{:S(2)}, u32[]{:S(2)}) async-start(f32[64,8,256]{2,1,0:T(8,128)} %shard_map.100), calls=%async_computation.1 | async-start | bytes 1048576 | tf_op jit(solution)/shard_map/all_to_all | solution.py:304
  42.2 20.3 %collective-permute-start = (f32[69,2,8,128]{3,2,1,0:T(8,128)S(1)}, f32[69,2,8,128]{3,2,1,0:T(8,128)S(1)}, u32[]{:S(2)}, u32[]{:S(2)}) collective-permute-start(f32[69,2,8,128]{3,2,1,0:T(8,128)S(1)} %get-tuple-element.14), channel_id=1, source_target_pairs={{0,1},{1,2},{2,3},{3,4},{4,5},{5,6},{6,7},{7,8},{8,9},{9,10},{10,1... | collective-permute-start | bytes 1695752 | tf_op jit(solution)/shard_map/ppermute | solution.py:300
  45.6 18.6 %collective-permute-start.1 = (f32[69,2,8,128]{3,2,1,0:T(8,128)S(1)}, f32[69,2,8,128]{3,2,1,0:T(8,128)S(1)}, u32[]{:S(2)}, u32[]{:S(2)}) collective-permute-start(f32[69,2,8,128]{3,2,1,0:T(8,128)S(1)} %get-tuple-element.15), channel_id=1, source_target_pairs={{1,0},{2,1},{3,2},{4,3},{5,4},{6,5},{7,6},{8,7},{9,8},{10,9},{11,1... | collective-permute-start | bytes 1695752 | tf_op jit(solution)/shard_map/ppermute | solution.py:300
  64.2 16.3 %copy-start.3 = (f32[5]{0:T(128)S(1)}, f32[5]{0:T(128)}, u32[]{:S(2)}) copy-start(f32[5]{0:T(128)} %weights.1) | copy-start | bytes 64
  69.5 6.7 %collective-permute-start.2 = (f32[50,8,128]{2,1,0:T(8,128)S(1)}, f32[50,8,128]{2,1,0:T(8,128)S(1)}, u32[]{:S(2)}, u32[]{:S(2)}) collective-permute-start(f32[50,8,128]{2,1,0:T(8,128)S(1)} %get-tuple-element.18.high), channel_id=1, source_target_pairs={{0,1},{1,2},{2,3},{3,4},{4,5},{5,6},{6,7},{7,8},{8,9},{9,10},{10,1... | collective-permute-start | bytes 614408 | tf_op jit(solution)/shard_map/ppermute | solution.py:300
  72.8 7.7 %collective-permute-start.3 = (f32[50,8,128]{2,1,0:T(8,128)S(1)}, f32[50,8,128]{2,1,0:T(8,128)S(1)}, u32[]{:S(2)}, u32[]{:S(2)}) collective-permute-start(f32[50,8,128]{2,1,0:T(8,128)S(1)} %get-tuple-element.19.low), channel_id=1, source_target_pairs={{1,0},{2,1},{3,2},{4,3},{5,4},{6,5},{7,6},{8,7},{9,8},{10,9},{11,1... | collective-permute-start | bytes 614408 | tf_op jit(solution)/shard_map/ppermute | solution.py:300
